TPU v7x, 32 devices: a whole 2x2x4 slice. The times are simulated.
32 devices in a mesh: rows: 8 (over z, x), grp: 4 (over y, core).
Axes of the slice: x: 2, y: 2, z: 4, core: 2. Of those that a mesh axis runs over, the one named last changes fastest.
Arguments:
- matrix: float32 [65536, 1024], P(('rows', 'grp'))
- row_signs: int32 [65536], P(('rows', 'grp')), may hold values from -1 to 1, as said below
- samples: int32 [8192], P(('rows', 'grp')), may hold values from 0 to 65535, as said below
Outputs:
- factor: float32 [1024, 1024], P('rows')
Inputs may be any that keep to these rules, and one draw needn't show every extreme that they name: `row_signs`: every entry is 1 or -1. `samples`: entries are distinct and increasing; entries k * 256 to (k + 1) * 256 - 1 lie in rows k * 2048 to (k + 1) * 2048 - 1.
All inputs are finite; a program needn't handle non-finite values.
Results may differ from a plain program's by a relative error of at most 0.00011.
Values sent between devices are 32-bit elements; how exact they have to be, the bound alone decides.
A program may use at most 128 MiB of HBM per device.

v0:
```python
import jax
import jax.numpy as jnp
from jax import lax
from jax.sharding import PartitionSpec as P

exact_mode = lax.Precision.HIGHEST


def parity_sign(left, right, length):
    correlation = left & right
    ones_total = jnp.zeros_like(correlation)
    for bit_level in range(max(1, length.bit_length() - 1)):
        ones_total = ones_total + (correlation >> bit_level & 1)
    return (1 - 2 * (ones_total % 2)).astype(jnp.float32)


def sylvester(length):
    indices = jnp.arange(length, dtype=jnp.int32)
    return parity_sign(indices[:, None], indices[None, :], length)


def shards(matrix, row_signs, samples):
    count_rows = lax.axis_size("rows")
    count_grp = lax.axis_size("grp")
    blocks = count_rows * count_grp
    row_dev, col_count = matrix.shape
    piece_rows = row_dev // blocks
    total_rows = row_dev * blocks
    sample_dev = samples.shape[0]
    position = lax.axis_index(("rows", "grp"))
    signed = matrix * row_signs.astype(jnp.float32)[:, None]
    before = jnp.dot(sylvester(row_dev), signed, precision=exact_mode)
    arrived = lax.all_to_all(
        lax.all_to_all(
            before.reshape(1, 1, row_dev, col_count),
            "rows",
            split_axis=2,
            concat_axis=0,
            tiled=True,
        ),
        "grp",
        split_axis=2,
        concat_axis=1,
        tiled=True,
    )
    mixed_rows = jnp.dot(
        sylvester(blocks), arrived.reshape(blocks, piece_rows * col_count), precision=exact_mode
    )
    mixed_rows = mixed_rows.reshape(count_rows, count_grp, piece_rows, col_count)
    mixed_rows = mixed_rows / jnp.sqrt(jnp.float32(total_rows))
    all_indices = lax.all_gather(samples, ("rows", "grp"), axis=0, tiled=True)
    owner_block = all_indices // row_dev
    within = all_indices % row_dev - position * piece_rows
    owner_hit = (owner_block[:, None] == jnp.arange(blocks, dtype=jnp.int32)[None, :]).astype(
        jnp.float32
    )
    local_hit = (within[:, None] == jnp.arange(piece_rows, dtype=jnp.int32)[None, :]).astype(
        jnp.float32
    )
    weights = jnp.einsum("kb,kt->bt", owner_hit, local_hit, precision=exact_mode).reshape(
        blocks * piece_rows
    )
    flat_rows = mixed_rows.reshape(blocks * piece_rows, col_count)
    local_gram = jnp.einsum(
        "kn,km->nm", flat_rows * weights[:, None], flat_rows, precision=exact_mode
    )
    summed_gram = lax.psum(local_gram, ("rows", "grp"))
    gram_total = summed_gram * (total_rows / (sample_dev * blocks))
    lower_factor = jnp.linalg.cholesky(gram_total)
    upper_factor = lower_factor.T
    share_rows = col_count // count_rows
    return lax.dynamic_slice_in_dim(
        upper_factor, lax.axis_index("rows") * share_rows, share_rows, 0
    )


def solution(mesh):
    return jax.shard_map(
        shards,
        mesh=mesh,
        in_specs=(P(("rows", "grp"), None), P(("rows", "grp")), P(("rows", "grp"))),
        out_specs=P("rows", None),
        check_vma=False,
    )
```

profile of v0, /device:TPU:0, one launch (start us, length us, event | category | flops | bytes accessed | tf_op | source)
XLA Modules:
  0.0 873.1 jit_solution(1184886997414699403)
XLA Ops:
  11.2 93.9 %fusion.26 = f32[1,1,2048,1024]{3,2,1,0:T(8,128)S(1)} fusion(f32[2048,1024]{1,0:T(8,128)S(1)} %fusion.115), kind=kOutput, calls=%fused_computation.29 | convolution fusion | flops 51736739840 | bytes 16777216 | tf_op jit(solution)/shard_map/dot_general | solution.py:32
  105.2 10.7 %copy.40 = f32[1,1,2048,1024]{3,1,0,2:T(1,128)S(1)} copy(f32[1,1,2048,1024]{3,2,1,0:T(8,128)S(1)} %fusion.26) | data formatting | bytes 16777216 | tf_op jit(solution)/shard_map/reshape | solution.py:35
  115.9 190.1 %all_to_all.21 = f32[1,1,2048,1024]{3,1,0,2:T(1,128)S(1)} all-to-all(f32[1,1,2048,1024]{3,1,0,2:T(1,128)S(1)} %copy.40), channel_id=1, replica_groups=mesh['rows'=8,'grp'=4] {'rows'}, dimensions={2} | all-to-all | bytes 16777216 | tf_op jit(solution)/shard_map/all_to_all | solution.py:34
  306.0 8.1 copy.41
  320.0 123.8 %all-gather = s32[32,1,256]{2,1,0:T(1,128)S(1)} all-gather(s32[1,1,256]{2,1,0:T(1,128)S(1)} %bitcast.77), channel_id=1, replica_groups=mesh['rows'=8,'grp'=4] {'rows','grp'}, dimensions={0}, use_global_device_ids=true | all-gather | bytes 33792 | tf_op jit(solution)/shard_map/all_gather | solution.py:51
  444.5 11.4 %copy.42 = f32[8,1,256,1024]{3,2,0,1:T(8,128)} copy(f32[8,1,256,1024]{3,0,1,2:T(8,128)} %all-to-all-done.1) | data formatting | bytes 16777216 | tf_op jit(solution)/shard_map/all_to_all | solution.py:33
  463.4 10.6 %fusion.9 = f32[8,4,64,1024]{3,0,2,1:T(8,128)S(1)} fusion(f32[4,64,8,1024]{3,2,1,0:T(8,128)} %bitcast.73, s32[8,4]{0,1:T(4,128)S(1)} %multiply_add_fusion), kind=kOutput, calls=%fused_computation.12 | convolution fusion | flops 805336064 | bytes 16777344 | tf_op jit(solution)/shard_map/dot_general | solution.py:46
  474.1 31.2 %fusion.35 = f32[1024,1024]{0,1:T(8,128)} fusion(f32[8,4,64,1024]{3,0,2,1:T(8,128)S(1)} %fusion.9, f32[8,4,64]{0,2,1:T(8,128)S(1)} %copy.44), kind=kOutput, calls=%fused_computation.35 | convolution fusion | flops 25773998080 | bytes 12591104 | tf_op jit(solution)/shard_map/kn,km->nm/dot_general | solution.py:64
  505.4 138.7 %all-reduce.3.cloned.1.call-done = f32[1024,1024]{0,1:T(8,128)} async-done(((f32[1024,1024]{0,1:T(8,128)}), f32[1024,1024]{0,1:T(8,128)}) %all-reduce.3.cloned.1.call-update) | async-done | bytes 4194320 | tf_op jit(solution)/shard_map/psum | solution.py:67
  660.8 11.7 %cholesky.223 = f32[128,128]{1,0:T(8,128)S(1)} custom-call(f32[128,128]{1,0:T(8,128)S(1)} %cholesky.580), custom_call_target="Cholesky" | custom-call | tf_op jit(solution)/shard_map/jit(cholesky)/cholesky | solution.py:69
  675.0 9.8 %custom-call.59 = f32[1,128,128]{1,2,0:T(8,128)S(1)} custom-call(f32[1,128,128]{2,1,0:T(8,128)S(1)} %get-tuple-element.26), custom_call_target="InvertDiagBlocksLowerTriangular" | custom-call | tf_op jit(solution)/shard_map/jit(cholesky)/cholesky | solution.py:69
  688.8 12.1 %cholesky.244 = f32[128,128]{1,0:T(8,128)S(1)} custom-call(f32[128,128]{1,0:T(8,128)S(1)} %cholesky.584), custom_call_target="Cholesky" | custom-call | tf_op jit(solution)/shard_map/jit(cholesky)/cholesky | solution.py:69
  701.5 9.8 %custom-call.60 = f32[1,128,128]{1,2,0:T(8,128)S(1)} custom-call(f32[1,128,128]{2,1,0:T(8,128)S(1)} %get-tuple-element.23), custom_call_target="InvertDiagBlocksLowerTriangular" | custom-call | tf_op jit(solution)/shard_map/jit(cholesky)/cholesky | solution.py:69
  714.7 11.7 %cholesky.468 = f32[128,128]{1,0:T(8,128)S(1)} custom-call(f32[128,128]{1,0:T(8,128)S(1)} %cholesky.589), custom_call_target="Cholesky" | custom-call | tf_op jit(solution)/shard_map/jit(cholesky)/cholesky | solution.py:69
  727.0 9.8 %custom-call.61 = f32[1,128,128]{1,2,0:T(8,128)S(1)} custom-call(f32[1,128,128]{2,1,0:T(8,128)S(1)} %get-tuple-element.20), custom_call_target="InvertDiagBlocksLowerTriangular" | custom-call | tf_op jit(solution)/shard_map/jit(cholesky)/cholesky | solution.py:69
  740.3 11.9 %cholesky.487 = f32[128,128]{1,0:T(8,128)S(1)} custom-call(f32[128,128]{1,0:T(8,128)S(1)} %cholesky.594), custom_call_target="Cholesky" | custom-call | tf_op jit(solution)/shard_map/jit(cholesky)/cholesky | solution.py:69
  752.9 9.8 %custom-call.62 = f32[1,128,128]{1,2,0:T(8,128)S(1)} custom-call(f32[1,128,128]{2,1,0:T(8,128)S(1)} %get-tuple-element.17), custom_call_target="InvertDiagBlocksLowerTriangular" | custom-call | tf_op jit(solution)/shard_map/jit(cholesky)/cholesky | solution.py:69
  766.1 11.7 %cholesky.506 = f32[128,128]{1,0:T(8,128)S(1)} custom-call(f32[128,128]{1,0:T(8,128)S(1)} %cholesky.599), custom_call_target="Cholesky" | custom-call | tf_op jit(solution)/shard_map/jit(cholesky)/cholesky | solution.py:69
  778.5 10.0 %custom-call.63 = f32[1,128,128]{1,2,0:T(8,128)S(1)} custom-call(f32[1,128,128]{2,1,0:T(8,128)S(1)} %get-tuple-element.14), custom_call_target="InvertDiagBlocksLowerTriangular" | custom-call | tf_op jit(solution)/shard_map/jit(cholesky)/cholesky | solution.py:69
  791.8 11.7 %cholesky.526 = f32[128,128]{1,0:T(8,128)S(1)} custom-call(f32[128,128]{1,0:T(8,128)S(1)} %cholesky.604), custom_call_target="Cholesky" | custom-call | tf_op jit(solution)/shard_map/jit(cholesky)/cholesky | solution.py:69
  804.2 9.8 %custom-call.64 = f32[1,128,128]{1,2,0:T(8,128)S(1)} custom-call(f32[1,128,128]{2,1,0:T(8,128)S(1)} %get-tuple-element.11), custom_call_target="InvertDiagBlocksLowerTriangular" | custom-call | tf_op jit(solution)/shard_map/jit(cholesky)/cholesky | solution.py:69
  817.0 11.7 %cholesky.546 = f32[128,128]{1,0:T(8,128)S(1)} custom-call(f32[128,128]{1,0:T(8,128)S(1)} %cholesky.609), custom_call_target="Cholesky" | custom-call | tf_op jit(solution)/shard_map/jit(cholesky)/cholesky | solution.py:69
  829.3 9.8 %custom-call.65 = f32[1,128,128]{1,2,0:T(8,128)S(1)} custom-call(f32[1,128,128]{2,1,0:T(8,128)S(1)} %get-tuple-element.8), custom_call_target="InvertDiagBlocksLowerTriangular" | custom-call | tf_op jit(solution)/shard_map/jit(cholesky)/cholesky | solution.py:69
  841.8 11.7 %cholesky.564 = f32[128,128]{1,0:T(8,128)S(1)} custom-call(f32[128,128]{1,0:T(8,128)S(1)} %convolution_subtract_fusion.6), custom_call_target="Cholesky" | custom-call | tf_op jit(solution)/shard_map/jit(cholesky)/cholesky | solution.py:69
  (57 shorter events, 72.3 us)
Async XLA Ops:
  314.1 5.9 copy-start.1
  314.1 130.4 %all-to-all-start.1 = ((f32[8,1,256,1024]{3,0,1,2:T(8,128)}), f32[8,1,256,1024]{3,0,1,2:T(8,128)}, u32[]{:S(2)}, u32[]{:S(2)}) async-start(f32[8,1,256,1024]{3,0,1,2:T(8,128)} %copy.41), calls=%async_computation.1 | async-start | bytes 16777216 | tf_op jit(solution)/shard_map/all_to_all | solution.py:33
  319.9 324.1 %all-reduce.3.cloned.1.call-start = ((), (), s32[]{:S(2)}) async-start(), calls=%async_computation.2 | async-start | bytes 8388608 | tf_op jit(solution)/shard_map/psum | solution.py:67
  658.8 1.9 copy-start
Sparse Core Ops, SparseCore 0:
  505.5 138.4 all-reduce.2
where the time goes:
time: 885 us; the launch traced here: 873 us
  blocking collectives  314 us (35%)
  other arithmetic  188 us (21%)
  matrix products  159 us (18%)
  waiting for transfers between devices  139 us (16%)
  local copies, waits for them, and re-layouts  48.6 us (5%)
  between operations  19.1 us (2%)
    all_to_all x1, blocking collectives, shards(): lax.all_to_all(before.reshape(1, 1, row_dev, col_count), 'rows', split_ax...  190 us
    another operation x30, other arithmetic, shards(): lower_factor = jnp.linalg.cholesky(gram_total)  172 us
    psum x1, waiting for transfers between devices, shards(): summed_gram = lax.psum(local_gram, ('rows', 'grp'))  139 us
    all_gather x1, blocking collectives, shards(): all_indices = lax.all_gather(samples, ('rows', 'grp'), axis=0, tiled=True)  124 us
    dot_general x1, matrix products, shards(): before = jnp.dot(sylvester(row_dev), signed, precision=exact_mode)  93.9 us
    dot_general x1, matrix products, shards(): jnp.einsum('kn,km->nm', flat_rows * weights[:, None], flat_rows, precisio...  31.2 us
    another operation x14, matrix products, shards(): lower_factor = jnp.linalg.cholesky(gram_total)  23.1 us
  transfers between devices with their start and end apart: 2, of which 1 were waited for; matrix products, arithmetic and copies ran while one was open for 0% of the time, Pallas kernels for 0%

commit v1 on v0

--- a/solution.py
+++ b/solution.py
@@ -64,7 +64,7 @@
     local_gram = jnp.einsum(
         "kn,km->nm", flat_rows * weights[:, None], flat_rows, precision=exact_mode
     )
-    summed_gram = lax.psum(local_gram, ("rows", "grp"))
+    summed_gram = lax.psum(lax.psum(local_gram, "grp"), "rows")
     gram_total = summed_gram * (total_rows / (sample_dev * blocks))
     lower_factor = jnp.linalg.cholesky(gram_total)
     upper_factor = lower_factor.T

time: 885 us -> 988 us (1.12)
  waiting for transfers between devices: 139 us -> 242 us
    psum x1 -> x2, waiting for transfers between devices: 139 us -> 242 us  [shards(): summed_gram = lax.psum(lax.psum(local_gram, 'grp'), 'rows')]
  transfers between devices with their start and end apart: 2 -> 3, of which waited for: 1 -> 2; matrix products, arithmetic and copies ran while one was open for 0% -> 0% of each run, Pallas kernels for 0% -> 0%
where the time goes in v1:
time: 988 us; the launch traced here: 976 us
  blocking collectives  314 us (32%)
  waiting for transfers between devices  242 us (24%)
  other arithmetic  188 us (19%)
  matrix products  159 us (16%)
  local copies, waits for them, and re-layouts  48.6 us (5%)
  between operations  19.1 us (2%)
    psum x2, waiting for transfers between devices, shards(): summed_gram = lax.psum(lax.psum(local_gram, 'grp'), 'rows')  242 us
    all_to_all x1, blocking collectives, shards(): lax.all_to_all(before.reshape(1, 1, row_dev, col_count), 'rows', split_ax...  190 us
    another operation x30, other arithmetic, shards(): lower_factor = jnp.linalg.cholesky(gram_total)  172 us
    all_gather x1, blocking collectives, shards(): all_indices = lax.all_gather(samples, ('rows', 'grp'), axis=0, tiled=True)  124 us
    dot_general x1, matrix products, shards(): before = jnp.dot(sylvester(row_dev), signed, precision=exact_mode)  93.9 us
    dot_general x1, matrix products, shards(): jnp.einsum('kn,km->nm', flat_rows * weights[:, None], flat_rows, precisio...  31.2 us
    another operation x14, matrix products, shards(): lower_factor = jnp.linalg.cholesky(gram_total)  23.1 us
  transfers between devices with their start and end apart: 3, of which 2 were waited for; matrix products, arithmetic and copies ran while one was open for 0% of the time, Pallas kernels for 0%

profile of v1, /device:TPU:0, one launch (start us, length us, event | category | flops | bytes accessed | tf_op | source)
XLA Modules:
  0.0 976.4 jit_solution(3706182834538380781)
XLA Ops:
  11.2 93.9 %fusion.26 = f32[1,1,2048,1024]{3,2,1,0:T(8,128)S(1)} fusion(f32[2048,1024]{1,0:T(8,128)S(1)} %fusion.115), kind=kOutput, calls=%fused_computation.29 | convolution fusion | flops 51736739840 | bytes 16777216 | tf_op jit(solution)/shard_map/dot_general | solution.py:32
  105.2 10.7 %copy.40 = f32[1,1,2048,1024]{3,1,0,2:T(1,128)S(1)} copy(f32[1,1,2048,1024]{3,2,1,0:T(8,128)S(1)} %fusion.26) | data formatting | bytes 16777216 | tf_op jit(solution)/shard_map/reshape | solution.py:35
  115.9 190.1 %all_to_all.21 = f32[1,1,2048,1024]{3,1,0,2:T(1,128)S(1)} all-to-all(f32[1,1,2048,1024]{3,1,0,2:T(1,128)S(1)} %copy.40), channel_id=1, replica_groups=mesh['rows'=8,'grp'=4] {'rows'}, dimensions={2} | all-to-all | bytes 16777216 | tf_op jit(solution)/shard_map/all_to_all | solution.py:34
  320.0 123.8 %all-gather = s32[32,1,256]{2,1,0:T(1,128)S(1)} all-gather(s32[1,1,256]{2,1,0:T(1,128)S(1)} %bitcast.77), channel_id=1, replica_groups=mesh['rows'=8,'grp'=4] {'rows','grp'}, dimensions={0}, use_global_device_ids=true | all-gather | bytes 33792 | tf_op jit(solution)/shard_map/all_gather | solution.py:51
  444.5 11.4 %copy.42 = f32[8,1,256,1024]{3,2,0,1:T(8,128)} copy(f32[8,1,256,1024]{3,0,1,2:T(8,128)} %all-to-all-done.1) | data formatting | bytes 16777216 | tf_op jit(solution)/shard_map/all_to_all | solution.py:33
  463.4 10.6 %fusion.9 = f32[8,4,64,1024]{3,0,2,1:T(8,128)S(1)} fusion(f32[4,64,8,1024]{3,2,1,0:T(8,128)} %bitcast.73, s32[8,4]{0,1:T(4,128)S(1)} %multiply_add_fusion), kind=kOutput, calls=%fused_computation.12 | convolution fusion | flops 805336064 | bytes 16777344 | tf_op jit(solution)/shard_map/dot_general | solution.py:46
  474.1 31.2 %fusion.35 = f32[1024,1024]{0,1:T(8,128)} fusion(f32[8,4,64,1024]{3,0,2,1:T(8,128)S(1)} %fusion.9, f32[8,4,64]{0,2,1:T(8,128)S(1)} %copy.44), kind=kOutput, calls=%fused_computation.35 | convolution fusion | flops 25773998080 | bytes 12591104 | tf_op jit(solution)/shard_map/kn,km->nm/dot_general | solution.py:64
  505.3 81.7 %all-reduce.4.cloned.1.call-done = f32[1024,1024]{0,1:T(8,128)} async-done(((f32[1024,1024]{0,1:T(8,128)}), f32[1024,1024]{0,1:T(8,128)}) %all-reduce.4.cloned.1.call-update) | async-done | bytes 4194320 | tf_op jit(solution)/shard_map/psum | solution.py:67
  587.1 160.2 %all-reduce.6.cloned.1.call-done = f32[1024,1024]{0,1:T(8,128)} async-done(((f32[1024,1024]{0,1:T(8,128)}), f32[1024,1024]{0,1:T(8,128)}) %all-reduce.6.cloned.1.call-update) | async-done | bytes 4194320 | tf_op jit(solution)/shard_map/psum | solution.py:67
  764.1 11.7 %cholesky.223 = f32[128,128]{1,0:T(8,128)S(1)} custom-call(f32[128,128]{1,0:T(8,128)S(1)} %cholesky.580), custom_call_target="Cholesky" | custom-call | tf_op jit(solution)/shard_map/jit(cholesky)/cholesky | solution.py:69
  778.3 9.8 %custom-call.59 = f32[1,128,128]{1,2,0:T(8,128)S(1)} custom-call(f32[1,128,128]{2,1,0:T(8,128)S(1)} %get-tuple-element.26), custom_call_target="InvertDiagBlocksLowerTriangular" | custom-call | tf_op jit(solution)/shard_map/jit(cholesky)/cholesky | solution.py:69
  792.1 12.1 %cholesky.244 = f32[128,128]{1,0:T(8,128)S(1)} custom-call(f32[128,128]{1,0:T(8,128)S(1)} %cholesky.584), custom_call_target="Cholesky" | custom-call | tf_op jit(solution)/shard_map/jit(cholesky)/cholesky | solution.py:69
  804.8 9.8 %custom-call.60 = f32[1,128,128]{1,2,0:T(8,128)S(1)} custom-call(f32[1,128,128]{2,1,0:T(8,128)S(1)} %get-tuple-element.23), custom_call_target="InvertDiagBlocksLowerTriangular" | custom-call | tf_op jit(solution)/shard_map/jit(cholesky)/cholesky | solution.py:69
  818.0 11.7 %cholesky.468 = f32[128,128]{1,0:T(8,128)S(1)} custom-call(f32[128,128]{1,0:T(8,128)S(1)} %cholesky.589), custom_call_target="Cholesky" | custom-call | tf_op jit(solution)/shard_map/jit(cholesky)/cholesky | solution.py:69
  830.3 9.8 %custom-call.61 = f32[1,128,128]{1,2,0:T(8,128)S(1)} custom-call(f32[1,128,128]{2,1,0:T(8,128)S(1)} %get-tuple-element.20), custom_call_target="InvertDiagBlocksLowerTriangular" | custom-call | tf_op jit(solution)/shard_map/jit(cholesky)/cholesky | solution.py:69
  843.7 11.9 %cholesky.487 = f32[128,128]{1,0:T(8,128)S(1)} custom-call(f32[128,128]{1,0:T(8,128)S(1)} %cholesky.594), custom_call_target="Cholesky" | custom-call | tf_op jit(solution)/shard_map/jit(cholesky)/cholesky | solution.py:69
  856.2 9.8 %custom-call.62 = f32[1,128,128]{1,2,0:T(8,128)S(1)} custom-call(f32[1,128,128]{2,1,0:T(8,128)S(1)} %get-tuple-element.17), custom_call_target="InvertDiagBlocksLowerTriangular" | custom-call | tf_op jit(solution)/shard_map/jit(cholesky)/cholesky | solution.py:69
  869.5 11.7 %cholesky.506 = f32[128,128]{1,0:T(8,128)S(1)} custom-call(f32[128,128]{1,0:T(8,128)S(1)} %cholesky.599), custom_call_target="Cholesky" | custom-call | tf_op jit(solution)/shard_map/jit(cholesky)/cholesky | solution.py:69
  881.8 10.0 %custom-call.63 = f32[1,128,128]{1,2,0:T(8,128)S(1)} custom-call(f32[1,128,128]{2,1,0:T(8,128)S(1)} %get-tuple-element.14), custom_call_target="InvertDiagBlocksLowerTriangular" | custom-call | tf_op jit(solution)/shard_map/jit(cholesky)/cholesky | solution.py:69
  895.2 11.7 %cholesky.526 = f32[128,128]{1,0:T(8,128)S(1)} custom-call(f32[128,128]{1,0:T(8,128)S(1)} %cholesky.604), custom_call_target="Cholesky" | custom-call | tf_op jit(solution)/shard_map/jit(cholesky)/cholesky | solution.py:69
  907.5 9.8 %custom-call.64 = f32[1,128,128]{1,2,0:T(8,128)S(1)} custom-call(f32[1,128,128]{2,1,0:T(8,128)S(1)} %get-tuple-element.11), custom_call_target="InvertDiagBlocksLowerTriangular" | custom-call | tf_op jit(solution)/shard_map/jit(cholesky)/cholesky | solution.py:69
  920.3 11.7 %cholesky.546 = f32[128,128]{1,0:T(8,128)S(1)} custom-call(f32[128,128]{1,0:T(8,128)S(1)} %cholesky.609), custom_call_target="Cholesky" | custom-call | tf_op jit(solution)/shard_map/jit(cholesky)/cholesky | solution.py:69
  932.7 9.8 %custom-call.65 = f32[1,128,128]{1,2,0:T(8,128)S(1)} custom-call(f32[1,128,128]{2,1,0:T(8,128)S(1)} %get-tuple-element.8), custom_call_target="InvertDiagBlocksLowerTriangular" | custom-call | tf_op jit(solution)/shard_map/jit(cholesky)/cholesky | solution.py:69
  945.1 11.7 %cholesky.564 = f32[128,128]{1,0:T(8,128)S(1)} custom-call(f32[128,128]{1,0:T(8,128)S(1)} %convolution_subtract_fusion.6), custom_call_target="Cholesky" | custom-call | tf_op jit(solution)/shard_map/jit(cholesky)/cholesky | solution.py:69
  (60 shorter events, 80.5 us)
Async XLA Ops:
  314.1 5.9 copy-start.1
  314.1 130.4 %all-to-all-start.1 = ((f32[8,1,256,1024]{3,0,1,2:T(8,128)}), f32[8,1,256,1024]{3,0,1,2:T(8,128)}, u32[]{:S(2)}, u32[]{:S(2)}) async-start(f32[8,1,256,1024]{3,0,1,2:T(8,128)} %copy.41), calls=%async_computation.1 | async-start | bytes 16777216 | tf_op jit(solution)/shard_map/all_to_all | solution.py:33
  319.9 267.2 %all-reduce.4.cloned.1.call-start = ((), (), s32[]{:S(2)}) async-start(), calls=%async_computation.2 | async-start | bytes 8388608 | tf_op jit(solution)/shard_map/psum | solution.py:67
  505.3 242.0 %all-reduce.6.cloned.1.call-start = ((), (), s32[]{:S(2)}) async-start(), calls=%async_computation.3 | async-start | bytes 8388608 | tf_op jit(solution)/shard_map/psum | solution.py:67
  762.1 1.9 copy-start
Sparse Core Ops, SparseCore 0:
  505.4 81.5 all-reduce.3
  590.7 156.5 all-reduce.5
